TPU v7x, 32 devices: a whole 2x2x4 slice. The times are simulated.
32 devices in a mesh: row: 4 (over x, core), col: 8 (over z, y).
Axes of the slice: x: 2, y: 2, z: 4, core: 2. Of those that a mesh axis runs over, the one named last changes fastest.
Arguments:
- centres: float32 [65536, 64], P(('row', 'col')), may hold values from -6 to 6
- weights: float32 [65536, 64], P(('row', 'col')), may hold values from -0.25 to 0.25
- targets: float32 [512, 64], replicated, may hold values from -6 to 6
- batch_index: int32 [512], replicated, may hold values from 0 to 65535
- nystrom_index: int32 [4096], replicated, may hold values from 0 to 65535
- eigvecs: float32 [4096, 1024], P('row', 'col'), may hold values from -0.09375 to 0.09375
- mode_scale: float32 [1024], P('col'), may hold values from 0.02 to 0.2
Outputs:
- residual: float32 [512, 64], replicated
- step: float32 [65536, 64], P(('row', 'col'))
All inputs are finite; a program needn't handle non-finite values.
Results may differ from a plain program's by a relative error of at most 0.0001.
Values sent between devices are 32-bit elements; how exact they have to be, the bound alone decides.
A program may use at most 128 MiB of HBM per device.

v0:
```python
import jax
import jax.numpy as jnp
from jax import lax
from jax.sharding import PartitionSpec as P

learning_rate = 0.25


def kernel(left, right):
    left_sq = jnp.sum(left * left, axis=1)
    right_sq = jnp.sum(right * right, axis=1)
    inner_prod = jnp.dot(
        left, right.T, precision=lax.Precision.HIGHEST, preferred_element_type=jnp.float32
    )
    return jnp.exp(
        -(left_sq[:, None] + right_sq[None, :] - 2.0 * inner_prod) / float(left.shape[1])
    )


def product(left, right):
    return jnp.dot(left, right, precision=lax.Precision.HIGHEST, preferred_element_type=jnp.float32)


def local(centres, weights, targets, batch_index, nystrom_index, eigvecs, mode_scale):
    rows_dev = centres.shape[0]
    block_rows = eigvecs.shape[0]
    offset = lax.axis_index(("row", "col")) * rows_dev

    def select_rows(index):
        local_rows = index - offset
        inside = (local_rows >= 0) & (local_rows < rows_dev)
        fetched = jnp.take(centres, jnp.clip(local_rows, 0, rows_dev - 1), axis=0)
        return jnp.where(inside[:, None], fetched, 0.0)

    batch_feats, nystrom = lax.psum(
        (select_rows(batch_index), select_rows(nystrom_index)), ("row", "col")
    )
    nys_block = lax.dynamic_slice_in_dim(nystrom, lax.axis_index("row") * block_rows, block_rows, 0)
    kern_batch = kernel(centres, batch_feats)
    partial_pred = lax.dot_general(
        kern_batch,
        weights,
        (((0,), (0,)), ((), ())),
        precision=lax.Precision.HIGHEST,
        preferred_element_type=jnp.float32,
    )
    prediction = lax.psum(partial_pred, ("row", "col"))
    residual = prediction - targets
    gradient = product(kernel(nys_block, batch_feats), residual)
    mode_terms = lax.dot_general(
        eigvecs,
        gradient,
        (((0,), (0,)), ((), ())),
        precision=lax.Precision.HIGHEST,
        preferred_element_type=jnp.float32,
    )
    coeff = mode_scale[:, None] * lax.psum(mode_terms, "row")
    correction = lax.psum(product(eigvecs, coeff), "col")
    direct = product(kern_batch, residual)
    folded = direct - product(
        kernel(centres, nystrom), lax.all_gather(correction, "row", axis=0, tiled=True)
    )
    step = learning_rate * folded
    return (residual, step)


def solution(mesh):
    in_specs = (
        P(("row", "col"), None),
        P(("row", "col"), None),
        P(),
        P(),
        P(),
        P("row", "col"),
        P("col"),
    )
    out_specs = (P(), P(("row", "col"), None))
    return jax.shard_map(local, mesh=mesh, in_specs=in_specs, out_specs=out_specs, check_vma=False)
```

profile of v0, /device:TPU:0, one launch (start us, length us, event | category | flops | bytes accessed | tf_op | source)
XLA Modules:
  0.0 467.1 jit_solution(167002956576013100)
XLA Ops:
  7.2 0.0 all-reduce.5.cloned.1.call-start
  7.2 0.7 compare_and_fusion.2
  8.0 1.4 copy.9
  9.4 1.0 gather_fusion
  10.4 0.9 select_select_fusion.1
  11.3 0.0 all-reduce.5.cloned.1.call-update
  11.4 0.0 all-reduce.9.cloned.1.call-start
  11.5 14.2 %gather_fusion.1 = f32[4096,64]{1,0:T(8,128)} fusion(f32[2048,64]{1,0:T(8,128)S(1)} %copy.9, s32[4096]{0:T(1024)S(1)} %fusion.30), kind=kCustom, calls=%fused_computation.1 | custom fusion | bytes 2113536 | tf_op jit(solution)/shard_map/jit(_take)/gather | solution.py:32
  25.7 6.0 %select_select_fusion = f32[4096,64]{1,0:T(8,128)} fusion(f32[4096,64]{1,0:T(8,128)} %gather_fusion.1, pred[4096]{0:T(1024)(128)(4,1)S(1)} %get-tuple-element.7, pred[4096]{0:T(1024)(128)(4,1)S(1)} %get-tuple-element.6), kind=kLoop, calls=%fused_computation.27 | loop fusion | flops 524288 | bytes 2105344 | tf_op jit(solution)/shard_map/jit(_where)/select_n | solution.py:33
  31.7 0.1 multiply_reduce_fusion.2
  31.8 111.6 %all-reduce.5.cloned.1.call-done = f32[512,64]{1,0:T(8,128)} async-done(((f32[512,64]{1,0:T(8,128)}), f32[512,64]{1,0:T(8,128)}) %all-reduce.5.cloned.1.call-update) | async-done | bytes 131088 | tf_op jit(solution)/shard_map/psum | solution.py:35
  143.3 1.1 multiply_reduce_fusion.3
  144.4 5.1 %fusion.13 = f32[2048,512]{0,1:T(8,128)S(1)} fusion(f32[512,64]{1,0:T(8,128)} %all-reduce.5.cloned.1.call-done, f32[2048,64]{0,1:T(8,128)S(1)} %copy-done.3, f32[512]{0:T(512)S(1)} %multiply_reduce_fusion.3, f32[2048]{0:T(1024)S(1)} %multiply_reduce_fusion.2), kind=kOutput, calls=%fused_computation.16 | convolution fusion | flops 810549248 | bytes 4859904 | tf_op jit(solution)/shard_map/dot_general | solution.py:12
  149.5 2.0 copy-done.1
  151.6 4.8 %fusion.36 = f32[512,64]{0,1:T(8,128)} fusion(f32[2048,512]{0,1:T(8,128)S(1)} %fusion.13, f32[2048,64]{0,1:T(8,128)S(1)} %copy-done.5), kind=kOutput, calls=%fused_computation.55 | convolution fusion | flops 805306368 | bytes 4849664 | tf_op jit(solution)/shard_map/dot_general | solution.py:40
  156.4 0.2 all-reduce.7.cloned.1.call-start
  156.7 134.4 %all-reduce.9.cloned.1.call-done = (f32[512,64]{0,1:T(8,128)}, f32[4096,64]{1,0:T(8,128)}) async-done(((f32[512,64]{0,1:T(8,128)}, f32[4096,64]{1,0:T(8,128)}), (f32[512,64]{0,1:T(8,128)}, f32[4096,64]{1,0:T(8,128)})) %all-reduce.9.cloned.1.call-update) | async-done | bytes 1179664 | tf_op jit(solution)/shard_map/psum | solution.py:47
  291.1 0.9 sub.30
  292.0 1.3 multiply_reduce_fusion.1
  293.3 2.8 fusion.26
  296.2 2.1 fusion.15
  298.3 1.0 convolution_bitcast_fusion.1
  299.3 10.7 %psum.38 = f32[128,64]{1,0:T(8,128)S(1)} all-reduce(f32[128,64]{1,0:T(8,128)S(1)} %convolution_bitcast_fusion.1), channel_id=1, replica_groups=mesh['row'=4,'col'=8] {'row'}, use_global_device_ids=true, to_apply=%region_7.8 | all-reduce | flops 8192 | bytes 65536 | tf_op jit(solution)/shard_map/psum | solution.py:57
  310.0 1.5 convolution_bitcast_fusion
  311.4 0.0 all-reduce.7.cloned.1.call-update
  311.5 0.3 all-gather.2.cloned.1.call-start
  311.8 0.6 multiply_reduce_fusion
  312.4 69.5 %all-reduce.7.cloned.1.call-done = f32[1024,64]{0,1:T(8,128)} async-done(((f32[1024,64]{0,1:T(8,128)}), f32[1024,64]{0,1:T(8,128)}) %all-reduce.7.cloned.1.call-update) | async-done | bytes 262160 | tf_op jit(solution)/shard_map/psum | solution.py:58
  381.9 0.0 all-gather.2.cloned.1.call-update
  381.9 30.2 %fusion.37 = f32[4096,2048]{0,1:T(8,128)} fusion(f32[4096,64]{1,0:T(8,128)S(1)} %copy-done.2, f32[2048,64]{0,1:T(8,128)S(1)} %copy-done.3), kind=kOutput, calls=%fused_computation.56 | convolution fusion | flops 6442450944 | bytes 35127296 | tf_op jit(solution)/shard_map/dot_general | solution.py:12
  412.1 42.7 %fusion.3 = f32[2048,64]{0,1:T(8,128)S(1)} fusion(f32[4096,64]{0,1:T(8,128)} %all-gather.2.cloned.1.call-done, f32[4096,2048]{0,1:T(8,128)} %fusion.37, f32[4096]{0:T(1024)S(1)} %multiply_reduce_fusion, f32[2048]{0:T(1024)S(1)} %multiply_reduce_fusion.2), kind=kOutput, calls=%fused_computation.6 | convolution fusion | flops 6484393984 | bytes 35151872 | tf_op jit(solution)/shard_map/dot_general | solution.py:21
  454.8 5.8 %fusion.14 = f32[2048,64]{0,1:T(8,128)} fusion(f32[2048,64]{0,1:T(8,128)S(1)} %fusion.3, f32[2048,512]{0,1:T(8,128)} %copy-done.1, f32[512,64]{0,1:T(8,128)S(1)} %sub.30), kind=kOutput, calls=%fused_computation.18 | convolution fusion | flops 805568512 | bytes 5373952 | tf_op jit(solution)/shard_map/dot_general | solution.py:21
  (24 shorter events, 0.1 us)
Async XLA Ops:
  7.2 291.1 %copy-start = (f32[1024,128]{1,0:T(8,128)S(1)}, f32[1024,128]{1,0:T(8,128)}, u32[]{:S(2)}) copy-start(f32[1024,128]{1,0:T(8,128)} %param.12) | copy-start | bytes 1572868
  7.2 136.2 %all-reduce.5.cloned.1.call-start = ((), (), s32[]{:S(2)}) async-start(), calls=%async_computation | async-start | bytes 524288 | tf_op jit(solution)/shard_map/psum | solution.py:35
  8.0 3.4 copy-start.8
  11.4 279.7 %all-reduce.9.cloned.1.call-start = ((), (), s32[]{:S(2)}) async-start(), calls=%async_computation.3 | async-start | bytes 4456448 | tf_op jit(solution)/shard_map/psum | solution.py:47
  25.7 6.0 %copy-start.3 = (f32[2048,64]{0,1:T(8,128)S(1)}, f32[2048,64]{0,1:T(8,128)}, u32[]{:S(2)}) copy-start(f32[2048,64]{0,1:T(8,128)} %param.7) | copy-start | bytes 1572868
  144.4 7.1 %copy-start.5 = (f32[2048,64]{0,1:T(8,128)S(1)}, f32[2048,64]{0,1:T(8,128)}, u32[]{:S(2)}) copy-start(f32[2048,64]{0,1:T(8,128)} %param.8) | copy-start | bytes 1572868
  149.5 2.0 copy-start.1
  156.4 134.7 %copy-start.7 = (f32[512,64]{0,1:T(8,128)S(1)}, f32[512,64]{0,1:T(8,128)}, u32[]{:S(2)}) copy-start(f32[512,64]{0,1:T(8,128)} %param.9) | copy-start | bytes 393220
  156.4 136.9 %copy-start.4 = (f32[512,64]{1,0:T(8,128)S(1)}, f32[512,64]{1,0:T(8,128)}, u32[]{:S(2)}) copy-start(f32[512,64]{1,0:T(8,128)} %all-reduce.5.cloned.1.call-done) | copy-start | bytes 393220
  156.4 225.5 %all-reduce.7.cloned.1.call-start = ((), (), s32[]{:S(2)}) async-start(), calls=%async_computation.1 | async-start | bytes 524288 | tf_op jit(solution)/shard_map/psum | solution.py:58
  292.0 162.8 %copy-start.6 = (f32[512,64]{0,1:T(8,128)}, f32[512,64]{0,1:T(8,128)S(1)}, u32[]{:S(2)}) copy-start(f32[512,64]{0,1:T(8,128)S(1)} %sub.30) | copy-start | bytes 393220
  296.2 13.8 %copy-start.9 = (f32[128]{0:T(128)S(1)}, f32[128]{0:T(128)}, u32[]{:S(2)}) copy-start(f32[128]{0:T(128)} %param.13) | copy-start | bytes 1540
  296.2 15.5 %copy-start.2 = (f32[4096,64]{1,0:T(8,128)S(1)}, f32[4096,64]{1,0:T(8,128)}, u32[]{:S(2)}) copy-start(f32[4096,64]{1,0:T(8,128)} %get-tuple-element.3) | copy-start | bytes 3145732
  311.5 100.6 %all-gather.2.cloned.1.call-start = ((), (), s32[]{:S(2)}) async-start(), calls=%async_computation.2 | async-start | bytes 1310720 | tf_op jit(solution)/shard_map/all_gather | solution.py:61
Sparse Core Ops, SparseCore 0:
  14.1 129.2 all-reduce.4
  156.6 134.4 all-reduce.8
  311.6 70.2 all-reduce.6
  383.3 15.8 all-gather.1
where the time goes:
time: 468 us; the launch traced here: 467 us
  waiting for transfers between devices  316 us (68%)
  matrix products  95.9 us (20%)
  local copies, waits for them, and re-layouts  18.7 us (4%)
  between operations  14 us (3%)
  other arithmetic  11.7 us (2%)
  blocking collectives  10.7 us (2%)
    psum x1, waiting for transfers between devices, local(): prediction = lax.psum(partial_pred, ('row', 'col'))  134 us
    psum x1, waiting for transfers between devices, local(): lax.psum((select_rows(batch_index), select_rows(nystrom_index)), ('row',...  112 us
    psum x1, waiting for transfers between devices, local(): correction = lax.psum(product(eigvecs, coeff), 'col')  69.5 us
    dot_general x4, matrix products, product(): jnp.dot(left, right, precision=lax.Precision.HIGHEST, preferred_element_t...  52 us
    dot_general x3, matrix products, kernel(): jnp.dot(left, right.T, precision=lax.Precision.HIGHEST, preferred_element...  38.1 us
    gather x2, local copies, waits for them, and re-layouts, select_rows(): fetched = jnp.take(centres, jnp.clip(local_rows, 0, rows_dev - 1), axis=0)  15.2 us
    psum x1, blocking collectives, local(): coeff = mode_scale[:, None] * lax.psum(mode_terms, 'row')  10.7 us
  transfers between devices with their start and end apart: 4, of which 3 were waited for; matrix products, arithmetic and copies ran while one was open for 11% of the time, Pallas kernels for 0%

commit v1 on v0

--- a/solution.py
+++ b/solution.py
@@ -4,6 +4,11 @@
 from jax.sharding import PartitionSpec as P
 
 learning_rate = 0.25
+
+
+def one_after_other(value, inner_axis, outer_axis):
+    partial = lax.psum(value, inner_axis)
+    return lax.psum(partial, outer_axis)
 
 
 def kernel(left, right):
@@ -32,8 +37,8 @@
         fetched = jnp.take(centres, jnp.clip(local_rows, 0, rows_dev - 1), axis=0)
         return jnp.where(inside[:, None], fetched, 0.0)
 
-    batch_feats, nystrom = lax.psum(
-        (select_rows(batch_index), select_rows(nystrom_index)), ("row", "col")
+    batch_feats, nystrom = one_after_other(
+        (select_rows(batch_index), select_rows(nystrom_index)), "col", "row"
     )
     nys_block = lax.dynamic_slice_in_dim(nystrom, lax.axis_index("row") * block_rows, block_rows, 0)
     kern_batch = kernel(centres, batch_feats)

time: 468 us -> 513 us (1.096)
  waiting for transfers between devices: 316 us -> 359 us
    psum x1 -> x2, waiting for transfers between devices: 112 us -> 169 us  [the longest x1 111 us: one_after_other(): partial = lax.psum(value, inner_axis)]
    psum x1, waiting for transfers between devices: 134 us -> 121 us  [local(): prediction = lax.psum(partial_pred, ('row', 'col'))]
  transfers between devices with their start and end apart: 4 -> 5, of which waited for: 3 -> 4; matrix products, arithmetic and copies ran while one was open for 11% -> 7% of each run, Pallas kernels for 0% -> 0%
where the time goes in v1:
time: 513 us
  waiting for transfers between devices  359 us (70%)
  matrix products  97.8 us (19%)
  local copies, waits for them, and re-layouts  18.6 us (4%)
  between operations  14 us (3%)
  other arithmetic  11.9 us (2%)
  blocking collectives  10.7 us (2%)
    psum x1, waiting for transfers between devices, local(): prediction = lax.psum(partial_pred, ('row', 'col'))  121 us
    psum x1, waiting for transfers between devices, one_after_other(): partial = lax.psum(value, inner_axis)  111 us
    psum x1, waiting for transfers between devices, local(): correction = lax.psum(product(eigvecs, coeff), 'col')  69.6 us
    psum x1, waiting for transfers between devices, one_after_other(): return lax.psum(partial, outer_axis)  57.1 us
    dot_general x4, matrix products, product(): jnp.dot(left, right, precision=lax.Precision.HIGHEST, preferred_element_t...  53.7 us
    dot_general x3, matrix products, kernel(): jnp.dot(left, right.T, precision=lax.Precision.HIGHEST, preferred_element...  38.3 us
    gather x2, local copies, waits for them, and re-layouts, select_rows(): fetched = jnp.take(centres, jnp.clip(local_rows, 0, rows_dev - 1), axis=0)  15.1 us
    psum x1, blocking collectives, local(): coeff = mode_scale[:, None] * lax.psum(mode_terms, 'row')  10.7 us
  transfers between devices with their start and end apart: 5, of which 4 were waited for; matrix products, arithmetic and copies ran while one was open for 7% of the time, Pallas kernels for 0%

profile of v1, /device:TPU:0, one launch (start us, length us, event | category | flops | bytes accessed | tf_op | source)
XLA Modules:
  0.0 512.9 jit_solution(337708901357331131)
XLA Ops:
  7.2 0.8 compare_and_fusion.1
  8.0 0.7 fusion.30
  8.8 0.7 compare_and_fusion.2
  9.5 1.4 copy.9
  10.8 1.0 gather_fusion
  11.9 14.1 %gather_fusion.1 = f32[4096,64]{1,0:T(8,128)} fusion(f32[2048,64]{1,0:T(8,128)S(1)} %copy.9, s32[4096]{0:T(1024)S(1)} %fusion.30), kind=kCustom, calls=%fused_computation.1 | custom fusion | bytes 2113536 | tf_op jit(solution)/shard_map/jit(_take)/gather | solution.py:37
  26.0 0.9 select_select_fusion.1
  26.9 5.9 %select_select_fusion = f32[4096,64]{1,0:T(8,128)} fusion(f32[4096,64]{1,0:T(8,128)} %gather_fusion.1, pred[4096]{0:T(1024)(128)(4,1)S(1)} %get-tuple-element.9, pred[4096]{0:T(1024)(128)(4,1)S(1)} %get-tuple-element.8), kind=kLoop, calls=%fused_computation.27 | loop fusion | flops 524288 | bytes 2105344 | tf_op jit(solution)/shard_map/jit(_where)/select_n | solution.py:38
  32.8 0.0 all-reduce.13.cloned.1.call-start
  32.9 111.5 %all-reduce.11.cloned.1.call-done = (f32[512,64]{1,0:T(8,128)}, f32[4096,64]{1,0:T(8,128)}) async-done(((f32[512,64]{1,0:T(8,128)}, f32[4096,64]{1,0:T(8,128)}), (f32[512,64]{1,0:T(8,128)}, f32[4096,64]{1,0:T(8,128)})) %all-reduce.11.cloned.1.call-update) | async-done | bytes 1179664 | tf_op jit(solution)/shard_map/psum | solution.py:10
  144.4 0.0 all-reduce.7.cloned.1.call-start
  144.4 0.1 multiply_reduce_fusion.2
  144.5 57.1 %all-reduce.13.cloned.1.call-done = (f32[512,64]{1,0:T(8,128)}, f32[4096,64]{1,0:T(8,128)}) async-done(((f32[512,64]{1,0:T(8,128)}, f32[4096,64]{1,0:T(8,128)}), (f32[512,64]{1,0:T(8,128)}, f32[4096,64]{1,0:T(8,128)})) %all-reduce.13.cloned.1.call-update) | async-done | bytes 1179664 | tf_op jit(solution)/shard_map/psum | solution.py:11
  201.6 1.1 multiply_reduce_fusion.3
  202.7 5.1 fusion.13
  207.8 2.0 copy-done.1
  209.8 4.8 fusion.36
  214.7 0.2 all-reduce.9.cloned.1.call-start
  215.0 3.1 fusion.26
  218.1 0.2 multiply_reduce_fusion.1
  218.3 121.1 %all-reduce.7.cloned.1.call-done = f32[512,64]{0,1:T(8,128)} async-done(((f32[512,64]{0,1:T(8,128)}), f32[512,64]{0,1:T(8,128)}) %all-reduce.7.cloned.1.call-update) | async-done | bytes 131088 | tf_op jit(solution)/shard_map/psum | solution.py:52
  339.4 0.9 sub.30
  340.4 3.7 fusion.15
  344.1 1.0 convolution_bitcast_fusion.1
  345.1 10.7 %psum.54 = f32[128,64]{1,0:T(8,128)S(1)} all-reduce(f32[128,64]{1,0:T(8,128)S(1)} %convolution_bitcast_fusion.1), channel_id=1, replica_groups=mesh['row'=4,'col'=8] {'row'}, use_global_device_ids=true, to_apply=%region_9.10 | all-reduce | flops 8192 | bytes 65536 | tf_op jit(solution)/shard_map/psum | solution.py:62
  355.9 1.5 convolution_bitcast_fusion
  357.4 0.3 all-gather.2.cloned.1.call-start
  357.6 0.6 multiply_reduce_fusion
  358.2 69.6 %all-reduce.9.cloned.1.call-done = f32[1024,64]{0,1:T(8,128)} async-done(((f32[1024,64]{0,1:T(8,128)}), f32[1024,64]{0,1:T(8,128)}) %all-reduce.9.cloned.1.call-update) | async-done | bytes 262160 | tf_op jit(solution)/shard_map/psum | solution.py:63
  427.8 30.1 %fusion.37 = f32[4096,2048]{0,1:T(8,128)} fusion(f32[4096,64]{1,0:T(8,128)S(1)} %copy-done.2, f32[2048,64]{0,1:T(8,128)S(1)} %copy-done.3), kind=kOutput, calls=%fused_computation.56 | convolution fusion | flops 6442450944 | bytes 35127296 | tf_op jit(solution)/shard_map/dot_general | solution.py:17
  457.9 42.7 %fusion.3 = f32[2048,64]{0,1:T(8,128)S(1)} fusion(f32[4096,64]{0,1:T(8,128)} %all-gather.2.cloned.1.call-done, f32[4096,2048]{0,1:T(8,128)} %fusion.37, f32[4096]{0:T(1024)S(1)} %multiply_reduce_fusion, f32[2048]{0:T(1024)S(1)} %multiply_reduce_fusion.2), kind=kOutput, calls=%fused_computation.6 | convolution fusion | flops 6484393984 | bytes 35151872 | tf_op jit(solution)/shard_map/dot_general | solution.py:26
  500.6 5.8 %fusion.14 = f32[2048,64]{0,1:T(8,128)} fusion(f32[2048,64]{0,1:T(8,128)S(1)} %fusion.3, f32[2048,512]{0,1:T(8,128)} %copy-done.1, f32[512,64]{0,1:T(8,128)S(1)} %sub.30), kind=kOutput, calls=%fused_computation.18 | convolution fusion | flops 805568512 | bytes 5373952 | tf_op jit(solution)/shard_map/dot_general | solution.py:26
  (25 shorter events, 0.2 us)
Async XLA Ops:
  7.2 336.9 %copy-start = (f32[1024,128]{1,0:T(8,128)S(1)}, f32[1024,128]{1,0:T(8,128)}, u32[]{:S(2)}) copy-start(f32[1024,128]{1,0:T(8,128)} %param.12) | copy-start | bytes 1572868
  7.2 137.2 %all-reduce.11.cloned.1.call-start = ((), (), s32[]{:S(2)}) async-start(), calls=%async_computation.3 | async-start | bytes 4718592 | tf_op jit(solution)/shard_map/psum | solution.py:10
  32.8 111.6 %copy-start.3 = (f32[2048,64]{0,1:T(8,128)S(1)}, f32[2048,64]{0,1:T(8,128)}, u32[]{:S(2)}) copy-start(f32[2048,64]{0,1:T(8,128)} %param.7) | copy-start | bytes 1572868
  32.8 168.8 %all-reduce.13.cloned.1.call-start = ((), (), s32[]{:S(2)}) async-start(), calls=%async_computation.4 | async-start | bytes 4718592 | tf_op jit(solution)/shard_map/psum | solution.py:11
  144.4 195.1 %all-reduce.7.cloned.1.call-start = ((), (), s32[]{:S(2)}) async-start(), calls=%async_computation | async-start | bytes 262144 | tf_op jit(solution)/shard_map/psum | solution.py:52
  202.7 7.1 %copy-start.5 = (f32[2048,64]{0,1:T(8,128)S(1)}, f32[2048,64]{0,1:T(8,128)}, u32[]{:S(2)}) copy-start(f32[2048,64]{0,1:T(8,128)} %param.8) | copy-start | bytes 1572868
  207.8 2.0 copy-start.1
  209.8 5.1 copy-start.2
  209.8 5.1 copy-start.4
  214.7 124.7 %copy-start.7 = (f32[512,64]{0,1:T(8,128)S(1)}, f32[512,64]{0,1:T(8,128)}, u32[]{:S(2)}) copy-start(f32[512,64]{0,1:T(8,128)} %param.9) | copy-start | bytes 393220
  214.7 213.1 %all-reduce.9.cloned.1.call-start = ((), (), s32[]{:S(2)}) async-start(), calls=%async_computation.1 | async-start | bytes 524288 | tf_op jit(solution)/shard_map/psum | solution.py:63
  340.4 160.3 %copy-start.6 = (f32[512,64]{0,1:T(8,128)}, f32[512,64]{0,1:T(8,128)S(1)}, u32[]{:S(2)}) copy-start(f32[512,64]{0,1:T(8,128)S(1)} %sub.30) | copy-start | bytes 393220
  340.4 15.5 %copy-start.8 = (f32[128]{0:T(128)S(1)}, f32[128]{0:T(128)}, u32[]{:S(2)}) copy-start(f32[128]{0:T(128)} %param.13) | copy-start | bytes 1540
  357.4 100.5 %all-gather.2.cloned.1.call-start = ((), (), s32[]{:S(2)}) async-start(), calls=%async_computation.2 | async-start | bytes 1310720 | tf_op jit(solution)/shard_map/all_gather | solution.py:66
Sparse Core Ops, SparseCore 0:
  33.0 111.3 all-reduce.10
  146.8 54.8 all-reduce.12
  214.8 124.5 all-reduce.6
  357.5 70.2 all-reduce.8
  429.2 15.8 all-gather.1
